TPU v7x, 32 devices: a whole 2x2x4 slice. The times are simulated.
32 devices in a mesh: dom: 32 (over z, y, x, core).
Axes of the slice: x: 2, y: 2, z: 4, core: 2. Of those that a mesh axis runs over, the one named last changes fastest.
Arguments:
- entities: float32 [32768, 200], P('dom'), may hold values from -3 to 3
- entity_state: float32 [32768], P('dom'), may hold values from 1e-05 to 0.1
- relations: float32 [1345, 200], replicated, may hold values from -3 to 3
- relation_state: float32 [1345], replicated, may hold values from 1 to 100
- edges: int32 [2, 3, 16384], P(None, None, 'dom'), may hold values from 0 to 1344, as said below
- negatives: int32 [2, 128, 1000], P(None, 'dom'), may hold values from 0 to 1023
- counts: int32 [2, 32], P(None, 'dom'), may hold values from 1 to 512, as said below
Outputs:
- entities_after: float32 [32768, 200], P('dom')
- entity_state_after: float32 [32768], P('dom')
- relations_after: float32 [1345, 200], replicated
- relation_state_after: float32 [1345], replicated
Inputs may be any that keep to these rules, and one draw needn't show every extreme that they name: `edges`: rows 0 and 2 are local entity ids below 1024; row 1 holds relation ids below 1345. `negatives`: local ids in the partner's partition. `counts`: in every round some bucket is full.
All inputs are finite; a program needn't handle non-finite values.
Results may differ from a plain program's by a relative error of at most 0.0003.
Values sent between devices are 32-bit elements; how exact they have to be, the bound alone decides.
A program may use at most 64 MiB of HBM per device.

v0:
```python
import jax
import jax.numpy as jnp
from jax import lax
from jax.sharding import PartitionSpec as P

RATE = 0.2
HIGH = lax.Precision.HIGHEST


def swapped(block, axis, apart):
    count = lax.axis_size(axis)
    route = []
    for low in range(count):
        high = low | 1 << apart
        if high != low and high < count:
            route += [(low, high), (high, low)]
    return lax.ppermute(block, axis, route)


def block_terms(carry, table, relations, source, relation, target, negative_ids, live):
    grad_table, grad_relation = carry
    half = table.shape[1] // 2
    src_rows = table[source]
    tgt_rows = table[target]
    neg_rows = table[negative_ids]
    rel_rows = relations[relation]
    src_real, src_imag = (src_rows[:, :half], src_rows[:, half:])
    rel_real, rel_imag = (rel_rows[:, :half], rel_rows[:, half:])
    product = jnp.concatenate(
        [src_real * rel_real - src_imag * rel_imag, src_real * rel_imag + src_imag * rel_real],
        axis=1,
    )
    positive = jnp.sum(product * tgt_rows, axis=1)
    negative = lax.dot_general(
        product,
        neg_rows,
        (((1,), (1,)), ((), ())),
        precision=HIGH,
        preferred_element_type=jnp.float32,
    )
    pos_weight = -jax.nn.sigmoid(-positive) * live
    neg_weight = jax.nn.sigmoid(negative) * (live[:, None] / negative.shape[1])
    upstream = pos_weight[:, None] * tgt_rows + jnp.dot(
        neg_weight, neg_rows, precision=HIGH, preferred_element_type=jnp.float32
    )
    target_grad = pos_weight[:, None] * product
    negative_grad = lax.dot_general(
        neg_weight,
        product,
        (((0,), (0,)), ((), ())),
        precision=HIGH,
        preferred_element_type=jnp.float32,
    )
    up_real, up_imag = (upstream[:, :half], upstream[:, half:])
    source_grad = jnp.concatenate(
        [up_real * rel_real + up_imag * rel_imag, up_imag * rel_real - up_real * rel_imag], axis=1
    )
    relation_grad = jnp.concatenate(
        [up_real * src_real + up_imag * src_imag, up_imag * src_real - up_real * src_imag], axis=1
    )
    grad_table = (
        grad_table.at[source]
        .add(source_grad)
        .at[target]
        .add(target_grad)
        .at[negative_ids]
        .add(negative_grad)
    )
    grad_relation = grad_relation.at[relation].add(relation_grad)
    return (grad_table, grad_relation)


def bucket_pass(
    carry,
    table,
    relations,
    edge_pair,
    negative_pair,
    count_pair,
    source_shift,
    target_shift,
    block,
    first,
    last,
):
    block_pair = (count_pair + block - 1) // block

    def visit(index, inner):
        which = (index >= block_pair[0]).astype(jnp.int32)
        number = index - which * block_pair[0]
        edge_list = lax.dynamic_index_in_dim(edge_pair, which, 0, keepdims=False)
        start = number * block
        window = lax.dynamic_slice_in_dim(edge_list, start, block, 1)
        negative_list = lax.dynamic_index_in_dim(negative_pair, which, 0, keepdims=False)
        negative_ids = (
            lax.dynamic_index_in_dim(negative_list, number, 0, keepdims=False) + target_shift[which]
        )
        live = (start + jnp.arange(block, dtype=jnp.int32) < count_pair[which]).astype(jnp.float32)
        return block_terms(
            inner,
            table,
            relations,
            window[0] + source_shift[which],
            window[1],
            window[2] + target_shift[which],
            negative_ids,
            live,
        )

    return lax.fori_loop(first, last, visit, carry)


def adagrad(param, state, grad):
    new_state = state + jnp.mean(grad * grad, axis=1)
    return (param - RATE * grad / jnp.sqrt(new_state)[:, None], new_state)


def body(entities, entity_state, relations, relation_state, edges, negatives, counts):
    rows = entities.shape[0]
    blocks_dev = negatives.shape[1]
    block = edges.shape[2] // blocks_dev
    levels = lax.axis_size("dom").bit_length() - 1
    for round_index, bit in enumerate((levels - 1, 0)):
        partner = swapped(entities, "dom", bit)
        table = jnp.concatenate([entities, partner], axis=0)
        own_edges = edges[round_index]
        own_negatives = negatives[round_index]
        own_count = counts[round_index]
        other_edges, other_negatives, other_count = swapped(
            (own_edges, own_negatives, own_count), "dom", bit
        )
        upper = lax.axis_index("dom") // 2**bit % 2
        flipped = upper == 1
        edge_pair = jnp.where(
            flipped, jnp.stack([other_edges, own_edges]), jnp.stack([own_edges, other_edges])
        )
        negative_pair = jnp.where(
            flipped,
            jnp.stack([other_negatives, own_negatives]),
            jnp.stack([own_negatives, other_negatives]),
        )
        count_pair = jnp.where(
            flipped,
            jnp.concatenate([other_count, own_count]),
            jnp.concatenate([own_count, other_count]),
        )
        source_shift = jnp.stack([upper * rows, (1 - upper) * rows])
        target_shift = jnp.stack([(1 - upper) * rows, upper * rows])
        block_pair = (count_pair + block - 1) // block
        total = block_pair[0] + block_pair[1]
        middle = (total + 1) // 2
        first = upper * middle
        last = middle + upper * (total - middle)
        empty = (
            jnp.zeros((2 * rows, entities.shape[1]), jnp.float32),
            jnp.zeros(relations.shape, jnp.float32),
        )
        grads, relation_grads = bucket_pass(
            empty,
            table,
            relations,
            edge_pair,
            negative_pair,
            count_pair,
            source_shift,
            target_shift,
            block,
            first,
            last,
        )
        returned = swapped(grads[rows:], "dom", bit)
        relation_total = lax.psum(relation_grads, "dom")
        entities, entity_state = adagrad(entities, entity_state, grads[:rows] + returned)
        relations, relation_state = adagrad(relations, relation_state, relation_total)
    return (entities, entity_state, relations, relation_state)


def solution(mesh):
    return jax.shard_map(
        body,
        mesh=mesh,
        in_specs=(
            P("dom", None),
            P("dom"),
            P(),
            P(),
            P(None, None, "dom"),
            P(None, "dom", None),
            P(None, "dom"),
        ),
        out_specs=(P("dom", None), P("dom"), P(), P()),
        check_vma=False,
    )
```

profile of v0, /device:TPU:0, one launch (start us, length us, event | category | flops | bytes accessed | tf_op | source)
XLA Modules:
  0.0 608.5 jit_solution(12843747475687905343)
XLA Ops:
  8.5 4.1 collective-permute-start
  14.0 2.9 collective-permute-start.1
  18.3 2.8 copy.91
  24.3 27.5 %collective-permute-done.1 = s32[3,512]{1,0:T(4,128)S(1)} collective-permute-done((s32[3,512]{1,0:T(4,128)S(1)}, s32[3,512]{1,0:T(4,128)S(1)}, u32[]{:S(2)}, u32[]{:S(2)}) %collective-permute-start.1) | collective-permute-done | bytes 6176 | tf_op jit(solution)/shard_map/ppermute | solution.py:17
  55.3 80.7 %while.30 = (s32[]{:T(128)}, f32[2048,200]{1,0:T(8,128)S(1)}, f32[1345,200]{1,0:T(8,128)}, s32[]{:T(128)}, s32[2]{0:T(128)S(1)}, /*index=5*/s32[2,3,512]{2,1,0:T...) while((s32[]{:T(128)}, f32[2048,200]{1,0:T(8,128)S(1)}, ...), condition=%wide.region_6.7_spmd, body=%wide.region_0.6_spmd.sunk | while | flops 922911104 | bytes 17251100 | solution.py:110
  61.8 2.4 gather_fusion.2
  64.3 2.3 gather_fusion
  68.3 5.2 gather_fusion.1
  80.7 4.0 scatter_fusion.3
  88.8 6.8 %scatter_fusion.2 = f32[2048,200]{1,0:T(8,128)S(1)} fusion(f32[2048,200]{1,0:T(8,128)S(1)} %scatter_fusion.1, s32[1000]{0:T(1024)S(1)} %bitcast.123, f32[1000,200]{1,0:T(8,128)S(1)} %fusion.66), kind=kCustom, calls=%fused_computation.10.clone.1 | custom fusion | flops 200000 | bytes 2404000 | tf_op jit(solution)/shard_map/while/body/scatter-add | solution.py:67
  102.2 2.4 gather_fusion.2
  108.6 5.2 gather_fusion.1
  121.0 4.0 scatter_fusion.3
  129.1 6.8 %scatter_fusion.2 = f32[2048,200]{1,0:T(8,128)S(1)} fusion(f32[2048,200]{1,0:T(8,128)S(1)} %scatter_fusion.1, s32[1000]{0:T(1024)S(1)} %bitcast.123, f32[1000,200]{1,0:T(8,128)S(1)} %fusion.66), kind=kCustom, calls=%fused_computation.10.clone.1 | custom fusion | flops 200000 | bytes 2404000 | tf_op jit(solution)/shard_map/while/body/scatter-add | solution.py:67
  148.7 20.0 %collective-permute-done.4 = f32[1024,200]{0,1:T(8,128)} collective-permute-done((f32[1024,200]{0,1:T(8,128)}, f32[1024,200]{0,1:T(8,128)}, u32[]{:S(2)}, u32[]{:S(2)}) %collective-permute-start.4) | collective-permute-done | bytes 819232 | tf_op jit(solution)/shard_map/ppermute | solution.py:17
  172.3 145.7 %all-reduce.3.cloned.1.call-done = f32[1345,200]{0,1:T(8,128)} async-done(((f32[1345,200]{0,1:T(8,128)}), f32[1345,200]{0,1:T(8,128)}) %all-reduce.3.cloned.1.call-update) | async-done | bytes 1076016 | tf_op jit(solution)/shard_map/psum | solution.py:172
  327.1 44.8 %while.31 = (s32[]{:T(128)}, f32[2048,200]{1,0:T(8,128)S(1)}, f32[1345,200]{1,0:T(8,128)}, s32[]{:T(128)}, s32[2]{0:T(128)}, /*index=5*/s32[2,3,512]{2,1,0:T(4,1...) while((s32[]{:T(128)}, f32[2048,200]{1,0:T(8,128)S(1)}, ...), condition=%wide.region_16.17_spmd, body=%wide.region_10.16_spmd.sunk | while | flops 922911104 | bytes 16896204 | solution.py:110
  338.2 2.4 gather_fusion.6
  340.7 2.3 gather_fusion.4
  344.6 5.2 gather_fusion.5
  357.0 4.0 scatter_fusion.7
  365.1 6.8 %scatter_fusion.6 = f32[2048,200]{1,0:T(8,128)S(1)} fusion(f32[2048,200]{1,0:T(8,128)S(1)} %scatter_fusion.5, s32[1000]{0:T(1024)S(1)} %bitcast.125, f32[1000,200]{1,0:T(8,128)S(1)} %fusion.75), kind=kCustom, calls=%fused_computation.14.clone.1 | custom fusion | flops 200000 | bytes 2404000 | tf_op jit(solution)/shard_map/while/body/scatter-add | solution.py:67
  371.9 2.8 copy.100
  377.9 216.9 %all-reduce.5.cloned.1.call-done = f32[1345,200]{0,1:T(8,128)} async-done(((f32[1345,200]{0,1:T(8,128)}), f32[1345,200]{0,1:T(8,128)}) %all-reduce.5.cloned.1.call-update) | async-done | bytes 1076016 | tf_op jit(solution)/shard_map/psum | solution.py:172
  (285 shorter events, 106.3 us)
Async XLA Ops:
  7.2 44.9 %copy-start.23 = (f32[1024,200]{0,1:T(8,128)S(1)}, f32[1024,200]{0,1:T(8,128)}, u32[]{:S(2)}) copy-start(f32[1024,200]{0,1:T(8,128)} %param.11) | copy-start | bytes 2457604
  7.2 310.9 %all-reduce.3.cloned.1.call-start = ((), (), s32[]{:S(2)}) async-start(), calls=%async_computation | async-start | bytes 2252800 | tf_op jit(solution)/shard_map/psum | solution.py:172
  8.5 12.6 %collective-permute-start = (s32[1]{0:T(128)}, s32[1]{0:T(128)}, u32[]{:S(2)}, u32[]{:S(2)}) collective-permute-start(s32[1]{0:T(128)} %bitcast.24), channel_id=1, source_target_pairs={{0,16},{16,0},{1,17},{17,1},{2,18},{18,2},{3,19},{19,3},{4,20},{20... | collective-permute-start | bytes 20 | tf_op jit(solution)/shard_map/ppermute | solution.py:17
  12.6 39.4 %collective-permute-start.2 = (f32[1024,200]{0,1:T(8,128)}, f32[1024,200]{0,1:T(8,128)S(1)}, u32[]{:S(2)}, u32[]{:S(2)}) collective-permute-start(f32[1024,200]{0,1:T(8,128)} %param.11), channel_id=1, source_target_pairs={{0,16},{16,0},{1,17},{17,1},{2,18},{18,2},{3,19},{19,3},{4,20},{20... | collective-permute-start | bytes 2457608 | tf_op jit(solution)/shard_map/ppermute | solution.py:17
  14.0 37.8 %collective-permute-start.1 = (s32[3,512]{1,0:T(4,128)S(1)}, s32[3,512]{1,0:T(4,128)S(1)}, u32[]{:S(2)}, u32[]{:S(2)}) collective-permute-start(s32[3,512]{1,0:T(4,128)S(1)} %bitcast.126), channel_id=1, source_target_pairs={{0,16},{16,0},{1,17},{17,1},{2,18},{18,2},{3,19},{19,3},{4,20},{20... | collective-permute-start | bytes 18440 | tf_op jit(solution)/shard_map/ppermute | solution.py:17
  18.3 33.8 %collective-permute-start.3 = (s32[4,1000]{1,0:T(4,128)S(1)}, s32[4,1000]{1,0:T(4,128)S(1)}, u32[]{:S(2)}, u32[]{:S(2)}) collective-permute-start(s32[4,1000]{1,0:T(4,128)S(1)} %get-tuple-element.543), channel_id=1, source_target_pairs={{0,16},{16,0},{1,17},{17,1},{2,18},{18,2},{3,19},{19,3},{4,20},{20... | collective-permute-start | bytes 48008 | tf_op jit(solution)/shard_map/ppermute | solution.py:17
  55.4 8.9 %copy-start.25 = (s32[2,4,1000]{2,1,0:T(4,128)}, s32[2,4,1000]{2,1,0:T(4,128)S(1)}, u32[]{:S(2)}) copy-start(s32[2,4,1000]{2,1,0:T(4,128)S(1)} %get-tuple-element.821) | copy-start | bytes 96004 | tf_op jit(solution)/shard_map/while
  88.7 6.9 %copy-start.26 = (s32[2,4,1000]{2,1,0:T(4,128)S(1)}, s32[2,4,1000]{2,1,0:T(4,128)}, u32[]{:S(2)}) copy-start(s32[2,4,1000]{2,1,0:T(4,128)} %copy-done.25) | copy-start | bytes 96004 | tf_op jit(solution)/shard_map/while
  95.7 8.9 %copy-start.25 = (s32[2,4,1000]{2,1,0:T(4,128)}, s32[2,4,1000]{2,1,0:T(4,128)S(1)}, u32[]{:S(2)}) copy-start(s32[2,4,1000]{2,1,0:T(4,128)S(1)} %get-tuple-element.821) | copy-start | bytes 96004 | tf_op jit(solution)/shard_map/while
  137.8 9.4 %copy-start.2 = (f32[1345,200]{1,0:T(8,128)S(1)}, f32[1345,200]{1,0:T(8,128)}, u32[]{:S(2)}) copy-start(f32[1345,200]{1,0:T(8,128)} %get-tuple-element.377) | copy-start | bytes 3228004
  140.0 28.7 %collective-permute-start.4 = (f32[1024,200]{0,1:T(8,128)}, f32[1024,200]{0,1:T(8,128)}, u32[]{:S(2)}, u32[]{:S(2)}) collective-permute-start(f32[1024,200]{0,1:T(8,128)} %slice.233), channel_id=1, source_target_pairs={{0,16},{16,0},{1,17},{17,1},{2,18},{18,2},{3,19},{19,3},{4,20},{20... | collective-permute-start | bytes 2457608 | tf_op jit(solution)/shard_map/ppermute | solution.py:17
  140.0 1.4 collective-permute-start.5
  140.0 5.9 collective-permute-start.6
  140.5 6.1 collective-permute-start.8
  147.2 21.5 %copy-start.17 = (f32[2048,200]{0,1:T(8,128)S(1)}, f32[2048,200]{0,1:T(8,128)}, u32[]{:S(2)}) copy-start(f32[2048,200]{0,1:T(8,128)} %copy.92) | copy-start | bytes 4915204
  148.6 21.4 %copy-start.34 = (f32[1024]{0:T(1024)S(1)}, f32[1024]{0:T(1024)}, u32[]{:S(2)}) copy-start(f32[1024]{0:T(1024)} %param.12) | copy-start | bytes 12292
  148.6 21.4 %copy-start.24 = (f32[1024,200]{0,1:T(8,128)S(1)}, f32[1024,200]{0,1:T(8,128)}, u32[]{:S(2)}) copy-start(f32[1024,200]{0,1:T(8,128)} %param.11) | copy-start | bytes 2457604
  148.6 446.1 %all-reduce.5.cloned.1.call-start = ((), (), s32[]{:S(2)}) async-start(), calls=%async_computation.1 | async-start | bytes 2252800 | tf_op jit(solution)/shard_map/psum | solution.py:172
  170.0 149.4 %copy-start.29 = (f32[1345]{0:T(1024)S(1)}, f32[1345]{0:T(1024)}, u32[]{:S(2)}) copy-start(f32[1345]{0:T(1024)} %param.14) | copy-start | bytes 16144
  172.3 147.1 %copy-start.21 = (f32[1345,200]{0,1:T(8,128)S(1)}, f32[1345,200]{0,1:T(8,128)}, u32[]{:S(2)}) copy-start(f32[1345,200]{0,1:T(8,128)} %param.13) | copy-start | bytes 3228004
  172.3 150.1 %collective-permute-start.7 = (f32[1024,200]{0,1:T(8,128)}, f32[1024,200]{0,1:T(8,128)}, u32[]{:S(2)}, u32[]{:S(2)}) collective-permute-start(f32[1024,200]{0,1:T(8,128)} %divide_subtract_fusion.3), channel_id=1, source_target_pairs={{0,1},{1,0},{2,3},{3,2},{4,5},{5,4},{6,7},{7,6},{8,9},{9,8},{10,11... | collective-permute-start | bytes 2457608 | tf_op jit(solution)/shard_map/ppermute | solution.py:17
  376.5 219.7 %copy-start.30 = (f32[1345]{0:T(1024)S(1)}, f32[1345]{0:T(1024)}, u32[]{:S(2)}) copy-start(f32[1345]{0:T(1024)} %param.14) | copy-start | bytes 16144
  376.5 220.3 %copy-start.20 = (f32[1345,200]{0,1:T(8,128)S(1)}, f32[1345,200]{0,1:T(8,128)}, u32[]{:S(2)}) copy-start(f32[1345,200]{0,1:T(8,128)} %copy-done.19) | copy-start | bytes 3228004
  377.8 220.2 %collective-permute-start.9 = (f32[1024,200]{0,1:T(8,128)S(1)}, f32[1024,200]{0,1:T(8,128)S(1)}, u32[]{:S(2)}, u32[]{:S(2)}) collective-permute-start(f32[1024,200]{0,1:T(8,128)S(1)} %slice.235), channel_id=1, source_target_pairs={{0,1},{1,0},{2,3},{3,2},{4,5},{5,4},{6,7},{7,6},{8,9},{9,8},{10,11... | collective-permute-start | bytes 2457608 | tf_op jit(solution)/shard_map/ppermute | solution.py:17
  (50 other events, 222.1 us)
Sparse Core Ops, SparseCore 0:
  148.8 169.2 all-reduce.2
  374.8 219.8 all-reduce.4
where the time goes:
time: 611 us; the launch traced here: 609 us
  waiting for transfers between devices  411 us (67%)
  local copies, waits for them, and re-layouts  79.5 us (13%)
  other arithmetic  74.5 us (12%)
  between operations  16.9 us (3%)
  matrix products  16.4 us (3%)
  starting transfers between devices  7.76 us (1%)
    psum x2, waiting for transfers between devices, body(): relation_total = lax.psum(relation_grads, 'dom')  363 us
    ppermute x10, waiting for transfers between devices, swapped(): return lax.ppermute(block, axis, route)  47.9 us
    scatter-add x9, other arithmetic, block_terms(): grad_table = grad_table.at[source].add(source_grad).at[target].add(target...  32.7 us
    while x8, local copies, waits for them, and re-layouts, bucket_pass(): return lax.fori_loop(first, last, visit, carry)  15.6 us
    gather x3, local copies, waits for them, and re-layouts, block_terms(): neg_rows = table[negative_ids]  15.5 us
  transfers between devices with their start and end apart: 12, of which 6 were waited for; matrix products, arithmetic and copies ran while one was open for 5% of the time, Pallas kernels for 0%

commit v1 on v0

--- a/solution.py
+++ b/solution.py
@@ -169,7 +169,7 @@
             last,
         )
         returned = swapped(grads[rows:], "dom", bit)
-        relation_total = lax.psum(relation_grads, "dom")
+        relation_total = jnp.sum(lax.all_gather(relation_grads, "dom"), axis=0)
         entities, entity_state = adagrad(entities, entity_state, grads[:rows] + returned)
         relations, relation_state = adagrad(relations, relation_state, relation_total)
     return (entities, entity_state, relations, relation_state)

time: 611 us -> 841 us (1.38)
  waiting for transfers between devices: 411 us -> 577 us
  other arithmetic: 74.5 us -> 108 us
  local copies, waits for them, and re-layouts: 79.5 us -> 110 us
    all_gather x0 -> x2, waiting for transfers between devices: none -> 515 us  [body(): relation_total = jnp.sum(lax.all_gather(relation_grads, 'dom'), axis=0)]
    psum x2 -> x0, waiting for transfers between devices: 363 us -> none  [body(): relation_total = lax.psum(relation_grads, 'dom')]
    reduce_sum x0 -> x2, other arithmetic: none -> 27 us  [body(): relation_total = jnp.sum(lax.all_gather(relation_grads, 'dom'), axis=0)]
    ppermute x10, waiting for transfers between devices: 47.9 us -> 62.4 us  [swapped(): return lax.ppermute(block, axis, route)]
    while x108 -> x58, local copies, waits for them, and re-layouts: 1.42 us -> 12.8 us
  transfers between devices with their start and end apart: 12 -> 12, of which waited for: 6 -> 6; matrix products, arithmetic and copies ran while one was open for 5% -> 3% of each run, Pallas kernels for 0% -> 0%
where the time goes in v1:
time: 841 us; the launch traced here: 837 us
  waiting for transfers between devices  577 us (69%)
  local copies, waits for them, and re-layouts  110 us (13%)
  other arithmetic  108 us (13%)
  between operations  16.9 us (2%)
  matrix products  14.3 us (2%)
  starting transfers between devices  8.75 us (1%)
    all_gather x2, waiting for transfers between devices, body(): relation_total = jnp.sum(lax.all_gather(relation_grads, 'dom'), axis=0)  515 us
    ppermute x10, waiting for transfers between devices, swapped(): return lax.ppermute(block, axis, route)  62.4 us
    scatter-add x9, other arithmetic, block_terms(): grad_table = grad_table.at[source].add(source_grad).at[target].add(target...  32.8 us
    reduce_sum x2, other arithmetic, body(): relation_total = jnp.sum(lax.all_gather(relation_grads, 'dom'), axis=0)  27 us
  transfers between devices with their start and end apart: 12, of which 6 were waited for; matrix products, arithmetic and copies ran while one was open for 3% of the time, Pallas kernels for 0%

profile of v1, /device:TPU:0, one launch (start us, length us, event | category | flops | bytes accessed | tf_op | source)
XLA Modules:
  0.0 836.8 jit_solution(1819038853900316490)
XLA Ops:
  8.6 4.1 collective-permute-start.3
  14.0 2.9 collective-permute-start
  20.6 30.8 %collective-permute-done = s32[1]{0:T(128)} collective-permute-done((s32[1]{0:T(128)}, s32[1]{0:T(128)}, u32[]{:S(2)}, u32[]{:S(2)}) %collective-permute-start) | collective-permute-done | bytes 36 | tf_op jit(solution)/shard_map/ppermute | solution.py:17
  61.0 106.5 %while.30 = (s32[]{:T(128)}, f32[2048,200]{1,0:T(8,128)S(1)}, f32[1345,200]{1,0:T(8,128)}, s32[]{:T(128)}, s32[2]{0:T(128)S(1)}, /*index=5*/s32[2,3,512]{2,1,0:T...) while((s32[]{:T(128)}, f32[2048,200]{1,0:T(8,128)S(1)}, ...), condition=%wide.region_6.7_spmd, body=%wide.region_0.6_spmd.sunk | while | flops 922911104 | bytes 24889796 | solution.py:110
  65.7 3.0 gather_fusion
  85.2 5.2 gather_fusion.1
  100.3 6.8 scatter_fusion.2
  110.3 4.0 scatter_fusion.3
  119.0 3.0 gather_fusion
  138.4 5.2 gather_fusion.1
  153.5 6.8 scatter_fusion.2
  163.6 4.0 scatter_fusion.3
  167.6 2.8 copy.91
  173.8 28.7 %collective-permute-done.4 = f32[1024,200]{0,1:T(8,128)S(1)} collective-permute-done((f32[1024,200]{0,1:T(8,128)S(1)}, f32[1024,200]{0,1:T(8,128)S(1)}, u32[]{:S(2)}, u32[]{:S(2)}) %collective-permute-start.4) | collective-permute-done | bytes 819232 | tf_op jit(solution)/shard_map/ppermute | solution.py:17
  212.5 2.8 copy.94
  215.4 216.1 %all-gather.7.cloned.1.call-done = f32[32,1345,200]{1,2,0:T(8,128)} async-done(((f32[1,1345,200]{1,2,0:T(8,128)}), f32[32,1345,200]{1,2,0:T(8,128)}) %all-gather.7.cloned.1.call-update) | async-done | bytes 34432016 | tf_op jit(solution)/shard_map/all_gather | solution.py:172
  431.5 13.5 %reduce_sum.81 = f32[1345,200]{0,1:T(8,128)} reduce(f32[32,1345,200]{1,2,0:T(8,128)} %all-gather.7.cloned.1.call-done, f32[]{:T(128)} %constant.415.clone.1), dimensions={0}, to_apply=%region_8.9 | reduce | flops 8339000 | bytes 35508004 | tf_op jit(solution)/shard_map/reduce_sum | solution.py:172
  450.1 50.8 %while.31 = (s32[]{:T(128)}, f32[2048,200]{1,0:T(8,128)S(1)}, f32[1345,200]{1,0:T(8,128)}, s32[]{:T(128)}, s32[2]{0:T(128)}, /*index=5*/s32[2,3,512]{2,1,0:T(4,1...) while((s32[]{:T(128)}, f32[2048,200]{1,0:T(8,128)S(1)}, ...), condition=%wide.region_16.17_spmd, body=%wide.region_10.16_spmd.sunk | while | flops 922911104 | bytes 20381008 | solution.py:110
  456.0 3.0 gather_fusion.4
  471.8 5.2 gather_fusion.5
  486.9 6.8 scatter_fusion.6
  497.0 4.0 scatter_fusion.7
  511.1 298.6 %all-gather.9.cloned.1.call-done = f32[32,1345,200]{1,2,0:T(8,128)} async-done(((f32[1,1345,200]{1,2,0:T(8,128)}), f32[32,1345,200]{1,2,0:T(8,128)}) %all-gather.9.cloned.1.call-update) | async-done | bytes 34432016 | tf_op jit(solution)/shard_map/all_gather | solution.py:172
  809.8 13.5 %reduce_sum.84 = f32[1345,200]{0,1:T(8,128)} reduce(f32[32,1345,200]{1,2,0:T(8,128)} %all-gather.9.cloned.1.call-done, f32[]{:T(128)} %constant.415.clone.1), dimensions={0}, to_apply=%region_18.19 | reduce | flops 8339000 | bytes 35508004 | tf_op jit(solution)/shard_map/reduce_sum | solution.py:172
  (241 shorter events, 147.0 us)
Async XLA Ops:
  7.2 424.3 %all-gather.7.cloned.1.call-start = ((), (), s32[]{:S(2)}) async-start(), calls=%async_computation | async-start | bytes 37171200 | tf_op jit(solution)/shard_map/all_gather | solution.py:172
  8.6 47.2 %collective-permute-start.3 = (s32[4,1000]{1,0:T(4,128)S(1)}, s32[4,1000]{1,0:T(4,128)S(1)}, u32[]{:S(2)}, u32[]{:S(2)}) collective-permute-start(s32[4,1000]{1,0:T(4,128)S(1)} %get-tuple-element.547), channel_id=1, source_target_pairs={{0,16},{16,0},{1,17},{17,1},{2,18},{18,2},{3,19},{19,3},{4,20},{20... | collective-permute-start | bytes 48008 | tf_op jit(solution)/shard_map/ppermute | solution.py:17
  12.6 43.8 %collective-permute-start.2 = (f32[1024,200]{0,1:T(8,128)}, f32[1024,200]{0,1:T(8,128)}, u32[]{:S(2)}, u32[]{:S(2)}) collective-permute-start(f32[1024,200]{0,1:T(8,128)} %param.11), channel_id=1, source_target_pairs={{0,16},{16,0},{1,17},{17,1},{2,18},{18,2},{3,19},{19,3},{4,20},{20... | collective-permute-start | bytes 2457608 | tf_op jit(solution)/shard_map/ppermute | solution.py:17
  14.0 37.4 %collective-permute-start = (s32[1]{0:T(128)}, s32[1]{0:T(128)}, u32[]{:S(2)}, u32[]{:S(2)}) collective-permute-start(s32[1]{0:T(128)} %bitcast.24), channel_id=1, source_target_pairs={{0,16},{16,0},{1,17},{17,1},{2,18},{18,2},{3,19},{19,3},{4,20},{20... | collective-permute-start | bytes 20 | tf_op jit(solution)/shard_map/ppermute | solution.py:17
  18.2 36.9 %collective-permute-start.1 = (s32[3,512]{1,0:T(4,128)S(1)}, s32[3,512]{1,0:T(4,128)S(1)}, u32[]{:S(2)}, u32[]{:S(2)}) collective-permute-start(s32[3,512]{1,0:T(4,128)S(1)} %bitcast.130), channel_id=1, source_target_pairs={{0,16},{16,0},{1,17},{17,1},{2,18},{18,2},{3,19},{19,3},{4,20},{20... | collective-permute-start | bytes 18440 | tf_op jit(solution)/shard_map/ppermute | solution.py:17
  61.0 16.5 %copy-start.2 = (f32[1345,200]{1,0:T(8,128)}, f32[1345,200]{1,0:T(8,128)S(1)}, u32[]{:S(2)}) copy-start(f32[1345,200]{1,0:T(8,128)S(1)} %get-tuple-element.823) | copy-start | bytes 3228004 | tf_op jit(solution)/shard_map/while
  100.3 6.9 copy-start.17
  107.1 7.2 copy-start.3
  114.3 16.5 %copy-start.2 = (f32[1345,200]{1,0:T(8,128)}, f32[1345,200]{1,0:T(8,128)S(1)}, u32[]{:S(2)}) copy-start(f32[1345,200]{1,0:T(8,128)S(1)} %get-tuple-element.823) | copy-start | bytes 3228004 | tf_op jit(solution)/shard_map/while
  153.5 6.9 copy-start.17
  160.4 7.2 copy-start.3
  170.4 639.4 %all-gather.9.cloned.1.call-start = ((), (), s32[]{:S(2)}) async-start(), calls=%async_computation.1 | async-start | bytes 37171200 | tf_op jit(solution)/shard_map/all_gather | solution.py:172
  172.3 30.2 %copy-start.14 = (f32[2048,200]{0,1:T(8,128)S(1)}, f32[2048,200]{0,1:T(8,128)}, u32[]{:S(2)}) copy-start(f32[2048,200]{0,1:T(8,128)} %copy.88) | copy-start | bytes 4915204
  172.3 30.3 %copy-start.26 = (f32[1024]{0:T(1024)S(1)}, f32[1024]{0:T(1024)}, u32[]{:S(2)}) copy-start(f32[1024]{0:T(1024)} %param.12) | copy-start | bytes 12292
  172.3 30.4 %copy-start.19 = (f32[1024,200]{0,1:T(8,128)S(1)}, f32[1024,200]{0,1:T(8,128)}, u32[]{:S(2)}) copy-start(f32[1024,200]{0,1:T(8,128)} %param.11) | copy-start | bytes 2457604
  173.7 28.8 %collective-permute-start.4 = (f32[1024,200]{0,1:T(8,128)S(1)}, f32[1024,200]{0,1:T(8,128)S(1)}, u32[]{:S(2)}, u32[]{:S(2)}) collective-permute-start(f32[1024,200]{0,1:T(8,128)S(1)} %slice.233), channel_id=1, source_target_pairs={{0,16},{16,0},{1,17},{17,1},{2,18},{18,2},{3,19},{19,3},{4,20},{20... | collective-permute-start | bytes 2457608 | tf_op jit(solution)/shard_map/ppermute | solution.py:17
  202.7 8.0 copy-start.22
  203.0 9.6 %copy-start.15 = (f32[1024,200]{0,1:T(8,128)}, f32[1024,200]{0,1:T(8,128)S(1)}, u32[]{:S(2)}) copy-start(f32[1024,200]{0,1:T(8,128)S(1)} %divide_subtract_fusion.3) | copy-start | bytes 2457604
  203.0 8.3 collective-permute-start.7
  203.1 2.5 collective-permute-start.5
  203.6 7.1 collective-permute-start.8
  203.6 6.4 collective-permute-start.6
  493.8 7.2 copy-start.5
  506.8 2.4 collective-permute-start.9
  (26 other events, 82.0 us)
Sparse Core Ops, SparseCore 0:
  170.5 260.9 all-gather.6
  503.8 305.8 all-gather.8
